TPU v7x, 256 devices: a whole 4x4x8 slice. The times are simulated.
256 devices in a mesh: sub: 64 (over x, z, core), crs: 4 (over y).
Axes of the slice: x: 4, y: 4, z: 8, core: 2. Of those that a mesh axis runs over, the one named last changes fastest.
Arguments:
- residual: float32 [256, 6, 3072], P('sub', None, 'crs'), may hold values from -6 to 6
- stiffness: float32 [256, 6, 3072], P('sub', None, 'crs'), may hold values from 0.1 to 10
- solid: int32 [256, 6, 16], P('sub', None, 'crs'), may hold values 0 or 1
- inverses: bfloat16 [256, 6, 192, 3072], P('sub', None, None, 'crs')
- coarse_basis: bfloat16 [256, 24, 6, 3072], P('sub', None, None, 'crs'), may hold values from -0.29882812 to 0.29882812
- assign: int32 [256], replicated, may hold values from 0 to 255, as said below
- corners: int32 [256, 8], P('sub'), may hold values from 0 to 255, as said below
- coarse_inverse: float32 [768, 768], P('crs')
Outputs:
- preconditioned: float32 [256, 6, 3072], P('sub', None, 'crs')
- inner_value: float32 [1], replicated
Inputs may be any that keep to these rules, and one draw needn't show every extreme that they name: assign is a permutation of the 256 subdomain numbers, set at run time by the load balancer, so a subdomain's neighbours may be held on any devices. corners[t, c] is the number of corner c = 4 cx + 2 cy + cz of subdomain assign[t], the grid vertex at its place plus (cx, cy, cz) taken periodically, under one fixed permutation of the 256 vertices.
All inputs are finite; a program needn't handle non-finite values. No bound on the sum of `solid` on one device may be relied on, other than what follows from the above.
Results may differ from a plain program's by a relative error of at most 0.0028.
Values sent between devices are 32-bit elements; how exact they have to be, the bound alone decides.
No kernel may reach another device: no remote copies, remote signals or barrier semaphores. Data moves between devices by JAX's collectives and lax.ppermute only.
A program may use at most 128 MiB of HBM per device.

v0:
```python
import jax
import jax.numpy as jnp
from jax import lax
from jax.sharding import PartitionSpec as P


def partner_rows(assign, subs):
    depth = subs // 16
    slots = jnp.arange(subs, dtype=jnp.int32)
    inverse = jnp.sum(
        slots[:, None] * (assign[:, None] == slots[None, :]).astype(jnp.int32), axis=0
    )
    coord_a = assign // (4 * depth)
    coord_b = assign // depth % 4
    coord_c = assign % depth

    def number(first, second, third):
        return (first * 4 + second) * depth + third

    neighbours = jnp.stack(
        [
            number((coord_a + 1) % 4, coord_b, coord_c),
            number(coord_a, (coord_b + 1) % 4, coord_c),
            number(coord_a, coord_b, (coord_c + 1) % depth),
            number((coord_a + 3) % 4, coord_b, coord_c),
            number(coord_a, (coord_b + 3) % 4, coord_c),
            number(coord_a, coord_b, (coord_c + depth - 1) % depth),
        ],
        axis=1,
    )
    partner_slot = jnp.sum(
        inverse[None, None, :] * (neighbours[:, :, None] == slots[None, None, :]).astype(jnp.int32),
        axis=2,
    )
    partner_face = jnp.array([3, 4, 5, 0, 1, 2], dtype=jnp.int32)
    return (partner_slot * 6 + partner_face[None, :]).reshape(-1)


def body(residual, stiffness, solid, inverses, coarse_basis, assign, corners, coarse_inverse):
    slots_here, faces, width_here = residual.shape
    patches_here = solid.shape[2]
    entries = width_here // patches_here
    columns = lax.axis_size("crs")
    subs = assign.shape[0]
    face_rows = slots_here * faces
    rows = partner_rows(assign, subs)
    position = lax.axis_index("sub")
    own_rows = lax.dynamic_slice_in_dim(rows, position * face_rows, face_rows)
    flat_r = residual.reshape(face_rows, -1)
    flat_k = stiffness.reshape(face_rows, -1)
    solid_f = jnp.repeat(solid.astype(jnp.float32), entries, axis=2)
    all_r, all_k = (
        lax.all_gather(flat_r, "sub", axis=0, tiled=True),
        lax.all_gather(flat_k, "sub", axis=0, tiled=True),
    )
    partner_k = all_k[own_rows]
    weight = flat_k / (flat_k + partner_k)
    weight_partner = partner_k / (flat_k + partner_k)
    restricted_flat = weight * (flat_r + all_r[own_rows])
    restricted = (solid_f * restricted_flat.reshape(residual.shape)).astype(jnp.bfloat16)
    blocks = inverses.reshape(slots_here, faces, entries, patches_here, entries)
    vectors = restricted.reshape(slots_here, faces, patches_here, entries)
    local = jnp.einsum(
        "sfipj,sfpj->sfpi", blocks, vectors, preferred_element_type=jnp.float32
    ).reshape(residual.shape)
    coarse_part = jnp.einsum(
        "scfk,sfk->sc", coarse_basis, restricted, preferred_element_type=jnp.float32
    )
    total_coarse = 3 * subs
    index = (3 * corners[:, :, None] + jnp.arange(3, dtype=jnp.int32)[None, None, :]).reshape(
        slots_here, 24
    )
    onehot = (index[:, :, None] == jnp.arange(total_coarse, dtype=jnp.int32)[None, None, :]).astype(
        jnp.float32
    )
    coarse_local = jnp.einsum("sc,scn->n", coarse_part, onehot, precision=lax.Precision.HIGHEST)
    coarse_residual = lax.psum(coarse_local, ("sub", "crs"))
    block_width = total_coarse // columns
    start = lax.axis_index("crs") * block_width
    block_part = lax.dynamic_slice_in_dim(coarse_residual, start, block_width)
    terms = jnp.dot(block_part, coarse_inverse, precision=lax.Precision.HIGHEST)
    coarse_solution = lax.psum(terms, "crs")
    corner_values = jnp.einsum(
        "scn,n->sc", onehot, coarse_solution, precision=lax.Precision.HIGHEST
    ).astype(jnp.bfloat16)
    correction = jnp.einsum(
        "sc,scfk->sfk", corner_values, coarse_basis, preferred_element_type=jnp.float32
    )
    solution = solid_f * (local + correction)
    flat_u = solution.reshape(face_rows, -1)
    all_u = lax.all_gather(flat_u, "sub", axis=0, tiled=True)
    averaged = weight * flat_u + weight_partner * all_u[own_rows]
    preconditioned = averaged.reshape(residual.shape)
    inner_value = lax.psum(jnp.sum(residual * preconditioned), ("sub", "crs")).reshape(1)
    return (preconditioned, inner_value)


def solution(mesh):
    return jax.shard_map(
        body,
        mesh=mesh,
        in_specs=(
            P("sub", None, "crs"),
            P("sub", None, "crs"),
            P("sub", None, "crs"),
            P("sub", None, None, "crs"),
            P("sub", None, None, "crs"),
            P(),
            P("sub", None),
            P("crs", None),
        ),
        out_specs=(P("sub", None, "crs"), P()),
        check_vma=False,
    )
```

profile of v0, /device:TPU:1, one launch (start us, length us, event | category | flops | bytes accessed | tf_op | source)
XLA Modules:
  0.0 431.3 jit_solution(17880507166367437837)
XLA Ops:
  7.2 0.0 copy-start
  7.2 0.0 all-gather.4.cloned.1.call-start
  7.2 1.0 copy.44
  8.2 0.6 reshape.60
  8.8 0.0 all-gather.4.cloned.1.call-update
  8.9 0.0 all-gather.6.cloned.1.call-start
  8.9 0.9 copy.47
  9.8 0.6 reshape.62
  10.5 0.0 all-gather.6.cloned.1.call-update
  10.5 0.0 all-gather.8.cloned.1.call-start
  10.5 0.7 fusion.12
  11.3 0.8 select_reduce_fusion.1
  12.1 0.5 select_reduce_fusion
  12.6 0.7 multiply_add_fusion
  13.3 0.1 copy.42
  13.5 0.1 add.184
  13.6 0.7 convert_element_type.12
  14.3 0.1 copy.45
  14.4 0.1 broadcast_in_dim.5
  14.5 0.1 reshape.61
  14.7 0.0 copy-start.4
  14.7 0.0 copy-start.1
  14.7 0.0 copy-start.2
  14.7 11.4 %copy.63 = bf16[4,6,192,768]{2,3,1,0:T(8,128)(2,1)} copy(bf16[4,6,192,768]{3,2,1,0:T(8,128)(2,1)} %param.12) | data formatting | bytes 14155776 | tf_op jit(solution)/shard_map/reshape | solution.py:61
  26.1 0.0 copy-done.4
  26.1 0.1 add.189
  26.2 0.1 add.190
  26.3 0.1 add.192
  26.4 0.1 compare_select_fusion
  26.4 68.0 %all-gather.4.cloned.1.call-done = f32[1536,768]{1,0:T(8,128)} async-done(((f32[24,768]{1,0:T(8,128)}), f32[1536,768]{1,0:T(8,128)}) %all-gather.4.cloned.1.call-update) | async-done | bytes 4718608 | tf_op jit(solution)/shard_map/all_gather | solution.py:54
  94.5 3.0 gather_fusion
  97.5 77.1 %all-gather.6.cloned.1.call-done = f32[1536,768]{1,0:T(8,128)} async-done(((f32[24,768]{1,0:T(8,128)}), f32[1536,768]{1,0:T(8,128)}) %all-gather.6.cloned.1.call-update) | async-done | bytes 4718608 | tf_op jit(solution)/shard_map/all_gather | solution.py:53
  174.5 3.0 gather_fusion.1
  177.5 0.0 copy-done.1
  177.5 0.0 copy-done.2
  177.5 0.1 fusion.3
  177.6 0.1 reshape.108
  177.7 0.0 copy-start.3
  177.7 5.1 %fusion.25 = f32[4,6,4,1,192]{4,3,2,1,0:T(1,128)S(1)} fusion(bf16[4,6,4,192,1]{3,4,2,1,0:T(2,128)(2,1)S(1)} %reshape.108, bf16[4,6,192,4,192]{2,4,3,1,0:T(8,128)(2,1)} %bitcast.41), kind=kOutput, calls=%fused_computation.85 | convolution fusion | flops 7077888 | bytes 7188480 | tf_op jit(solution)/shard_map/sfipj,sfpj->sfpi/dot_general | solution.py:63
  182.9 0.1 reshape.65
  183.0 0.0 copy-done
  183.0 0.4 convolution_bitcast_fusion
  183.4 0.3 convolution_reduce_fusion.1
  183.7 75.2 %psum.21 = f32[768]{0:T(1024)S(1)} all-reduce(f32[768]{0:T(1024)S(1)} %convolution_reduce_fusion.1), channel_id=1, replica_groups=mesh['sub'=64,'crs'=4] {'sub','crs'}, use_global_device_ids=true, to_apply=%region_2.3 | all-reduce | flops 768 | bytes 6144 | tf_op jit(solution)/shard_map/psum | solution.py:77
  258.9 0.1 dynamic_slice.7
  259.0 0.0 copy-done.3
  259.0 0.4 convolution_reduce_fusion
  259.4 7.2 %psum.22 = f32[768]{0:T(1024)S(1)} all-reduce(f32[768]{0:T(1024)S(1)} %convolution_reduce_fusion), channel_id=1, replica_groups=mesh['sub'=64,'crs'=4] {'crs'}, use_global_device_ids=true, to_apply=%region_3.4 | all-reduce | flops 768 | bytes 6144 | tf_op jit(solution)/shard_map/psum | solution.py:82
  266.6 0.5 fusion
  267.2 0.3 fusion.7
  267.5 0.6 reshape.66
  268.1 0.0 all-gather.8.cloned.1.call-update
  268.2 77.2 %all-gather.8.cloned.1.call-done = f32[1536,768]{1,0:T(8,128)} async-done(((f32[24,768]{1,0:T(8,128)}), f32[1536,768]{1,0:T(8,128)}) %all-gather.8.cloned.1.call-update) | async-done | bytes 4718608 | tf_op jit(solution)/shard_map/all_gather | solution.py:91
  345.4 3.0 gather_fusion.2
  348.3 0.7 multiply_reduce_fusion
  349.0 0.7 copy.53
  349.7 75.1 %psum.23 = f32[1]{0:T(128)} all-reduce(f32[1]{0:T(128)} %bitcast.18), channel_id=1, replica_groups=mesh['sub'=64,'crs'=4] {'sub','crs'}, use_global_device_ids=true, to_apply=%region_5.6 | all-reduce | flops 1 | bytes 8 | tf_op jit(solution)/shard_map/psum | solution.py:94
  (13 shorter events, 0.2 us)
Async XLA Ops:
  7.2 175.8 %copy-start = (bf16[4,24,6,768]{3,1,2,0:T(8,128)(2,1)S(1)}, bf16[4,24,6,768]{3,1,2,0:T(8,128)(2,1)}, u32[]{:S(2)}) copy-start(bf16[4,24,6,768]{3,1,2,0:T(8,128)(2,1)} %param.13) | copy-start | bytes 2654212
  7.2 87.3 %all-gather.4.cloned.1.call-start = ((), (), s32[]{:S(2)}) async-start(), calls=%async_computation | async-start | bytes 4792320 | tf_op jit(solution)/shard_map/all_gather | solution.py:54
  8.9 165.7 %all-gather.6.cloned.1.call-start = ((), (), s32[]{:S(2)}) async-start(), calls=%async_computation.1 | async-start | bytes 4792320 | tf_op jit(solution)/shard_map/all_gather | solution.py:53
  10.5 334.9 %all-gather.8.cloned.1.call-start = ((), (), s32[]{:S(2)}) async-start(), calls=%async_computation.2 | async-start | bytes 4792320 | tf_op jit(solution)/shard_map/all_gather | solution.py:91
  14.7 11.4 %copy-start.4 = (s32[4,8]{1,0:T(4,128)S(1)}, s32[4,8]{1,0:T(4,128)}, u32[]{:S(2)}) copy-start(s32[4,8]{1,0:T(4,128)} %param.15) | copy-start | bytes 388
  14.7 162.9 %copy-start.1 = (f32[4,6,768]{2,0,1:T(4,128)S(1)}, f32[4,6,768]{2,0,1:T(4,128)}, u32[]{:S(2)}) copy-start(f32[4,6,768]{2,0,1:T(4,128)} %param.9) | copy-start | bytes 221188
  14.7 162.9 %copy-start.2 = (f32[4,6,768]{2,0,1:T(4,128)S(1)}, f32[4,6,768]{2,0,1:T(4,128)}, u32[]{:S(2)}) copy-start(f32[4,6,768]{2,0,1:T(4,128)} %param.10) | copy-start | bytes 221188
  177.7 81.3 %copy-start.3 = (f32[192,768]{1,0:T(8,128)S(1)}, f32[192,768]{1,0:T(8,128)}, u32[]{:S(2)}) copy-start(f32[192,768]{1,0:T(8,128)} %param.16) | copy-start | bytes 1769476
Sparse Core Ops, SparseCore 0:
  10.8 83.6 all-gather.3
  97.8 76.6 all-gather.5
  268.3 77.0 all-gather.7
where the time goes:
time: 432 us; the launch traced here: 431 us
  waiting for transfers between devices  222 us (51%)
  blocking collectives  158 us (37%)
  local copies, waits for them, and re-layouts  26 us (6%)
  between operations  14 us (3%)
  matrix products  7.02 us (2%)
    all_gather x1, waiting for transfers between devices, body(): all_u = lax.all_gather(flat_u, 'sub', axis=0, tiled=True)  77.2 us
    all_gather x1, waiting for transfers between devices, body(): lax.all_gather(flat_r, 'sub', axis=0, tiled=True)  77.1 us
    psum x1, blocking collectives, body(): coarse_residual = lax.psum(coarse_local, ('sub', 'crs'))  75.2 us
    psum x1, blocking collectives, body(): lax.psum(jnp.sum(residual * preconditioned), ('sub', 'crs')).reshape(1)  75.1 us
    all_gather x1, waiting for transfers between devices, body(): lax.all_gather(flat_k, 'sub', axis=0, tiled=True)  68 us
    reshape x1, local copies, waits for them, and re-layouts, body(): blocks = inverses.reshape(slots_here, faces, entries, patches_here, entries)  11.4 us
  transfers between devices with their start and end apart: 3, of which 3 were waited for; matrix products, arithmetic and copies ran while one was open for 5% of the time, Pallas kernels for 0%

commit v1 on v0

--- a/solution.py
+++ b/solution.py
@@ -51,7 +51,9 @@
     solid_f = jnp.repeat(solid.astype(jnp.float32), entries, axis=2)
     all_r, all_k = (
         lax.all_gather(flat_r, "sub", axis=0, tiled=True),
-        lax.all_gather(flat_k, "sub", axis=0, tiled=True),
+        jnp.concatenate(
+            lax.all_to_all(jnp.stack([flat_k] * lax.axis_size("sub")), "sub", 0, 0), axis=0
+        ),
     )
     partner_k = all_k[own_rows]
     weight = flat_k / (flat_k + partner_k)

time: 432 us -> 405 us (0.938)
  waiting for transfers between devices: 222 us -> 183 us
  starting transfers between devices: 0.12 us -> 13.4 us
    all_to_all x0 -> x1, waiting for transfers between devices: none -> 107 us  [body(): lax.all_to_all(jnp.stack([flat_k] * lax.axis_size('sub')), 'sub', 0, 0)]
    all_gather x1, waiting for transfers between devices: 77.1 us -> 0.02 us  [body(): lax.all_gather(flat_r, 'sub', axis=0, tiled=True)]
    all_gather x1 -> x0, waiting for transfers between devices: 68 us -> none  [body(): lax.all_gather(flat_k, 'sub', axis=0, tiled=True)]
    all_to_all x0 -> x1, starting transfers between devices: none -> 13.3 us  [body(): lax.all_to_all(jnp.stack([flat_k] * lax.axis_size('sub')), 'sub', 0, 0)]
  transfers between devices with their start and end apart: 3 -> 3, of which waited for: 3 -> 2; matrix products, arithmetic and copies ran while one was open for 5% -> 4% of each run, Pallas kernels for 0% -> 0%
where the time goes in v1:
time: 405 us; the launch traced here: 404 us
  waiting for transfers between devices  183 us (45%)
  blocking collectives  158 us (39%)
  local copies, waits for them, and re-layouts  27 us (7%)
  between operations  14.3 us (4%)
  starting transfers between devices  13.4 us (3%)
  matrix products  7.01 us (2%)
    all_to_all x1, waiting for transfers between devices, body(): lax.all_to_all(jnp.stack([flat_k] * lax.axis_size('sub')), 'sub', 0, 0)  107 us
    all_gather x1, waiting for transfers between devices, body(): all_u = lax.all_gather(flat_u, 'sub', axis=0, tiled=True)  76.1 us
    psum x1, blocking collectives, body(): coarse_residual = lax.psum(coarse_local, ('sub', 'crs'))  76.1 us
    psum x1, blocking collectives, body(): lax.psum(jnp.sum(residual * preconditioned), ('sub', 'crs')).reshape(1)  75.2 us
    all_to_all x1, starting transfers between devices, body(): lax.all_to_all(jnp.stack([flat_k] * lax.axis_size('sub')), 'sub', 0, 0)  13.3 us
    reshape x1, local copies, waits for them, and re-layouts, body(): blocks = inverses.reshape(slots_here, faces, entries, patches_here, entries)  11.4 us
  transfers between devices with their start and end apart: 3, of which 2 were waited for; matrix products, arithmetic and copies ran while one was open for 4% of the time, Pallas kernels for 0%

profile of v1, /device:TPU:1, one launch (start us, length us, event | category | flops | bytes accessed | tf_op | source)
XLA Modules:
  0.0 404.4 jit_solution(1867476545099449818)
XLA Ops:
  7.2 0.0 copy-start
  7.2 1.0 copy.43
  8.2 2.5 stack.24
  10.6 0.0 copy-start.1
  10.7 0.0 copy-start.5
  10.7 0.0 copy-start.7
  10.7 0.0 copy-start.4
  10.7 13.3 %all-to-all-start = ((f32[64,24,768]{2,1,0:T(8,128)}), f32[64,24,768]{2,1,0:T(8,128)}, u32[]{:S(2)}, u32[]{:S(2)}) async-start(f32[64,24,768]{2,1,0:T(8,128)} %stack.24), calls=%async_computation | async-start | bytes 9437184 | tf_op jit(solution)/shard_map/all_to_all | solution.py:55
  24.0 0.0 all-gather.3.cloned.1.call-start
  24.0 0.0 copy-done.1
  24.1 0.6 reshape.65
  24.7 0.0 all-gather.3.cloned.1.call-update
  24.7 0.0 all-gather.5.cloned.1.call-start
  24.8 0.0 copy-done.5
  24.9 0.1 select_reduce_fusion.1
  25.0 0.5 select_reduce_fusion
  25.5 0.0 copy-done.7
  25.5 0.1 multiply_add_fusion
  25.6 0.1 copy.41
  25.7 0.1 add.184
  25.9 0.0 copy-done.4
  25.9 0.1 copy.44
  26.0 0.1 broadcast_in_dim.5
  26.1 0.1 reshape.64
  26.2 0.0 copy-start.6
  26.2 0.0 copy-start.2
  26.2 11.4 %copy.62 = bf16[4,6,192,768]{2,3,1,0:T(8,128)(2,1)} copy(bf16[4,6,192,768]{3,2,1,0:T(8,128)(2,1)} %param.12) | data formatting | bytes 14155776 | tf_op jit(solution)/shard_map/reshape | solution.py:63
  37.6 0.0 copy-done.6
  37.6 0.1 add.189
  37.7 0.1 add.190
  37.8 0.1 add.192
  37.9 0.1 compare_select_fusion
  38.0 107.0 %all-to-all-done = f32[64,24,768]{2,1,0:T(8,128)} async-done(((f32[64,24,768]{2,1,0:T(8,128)}), f32[64,24,768]{2,1,0:T(8,128)}, u32[]{:S(2)}, u32[]{:S(2)}) %all-to-all-start) | async-done | bytes 4718624 | tf_op jit(solution)/shard_map/all_to_all | solution.py:55
  144.9 3.0 gather_fusion
  147.9 0.0 all-gather.3.cloned.1.call-done
  147.9 3.0 gather_fusion.1
  150.9 0.0 copy-done.2
  150.9 0.1 fusion.3
  151.0 0.1 reshape.111
  151.1 0.0 copy-start.3
  151.1 5.1 %fusion.25 = f32[4,6,4,1,192]{4,3,2,1,0:T(1,128)S(1)} fusion(bf16[4,6,4,192,1]{3,4,2,1,0:T(2,128)(2,1)S(1)} %reshape.111, bf16[4,6,192,4,192]{2,4,3,1,0:T(8,128)(2,1)} %bitcast.42), kind=kOutput, calls=%fused_computation.85 | convolution fusion | flops 7077888 | bytes 7188480 | tf_op jit(solution)/shard_map/sfipj,sfpj->sfpi/dot_general | solution.py:65
  156.3 0.1 reshape.68
  156.4 0.0 copy-done
  156.4 0.4 convolution_bitcast_fusion
  156.8 0.3 convolution_reduce_fusion.1
  157.1 76.1 %psum.21 = f32[768]{0:T(1024)S(1)} all-reduce(f32[768]{0:T(1024)S(1)} %convolution_reduce_fusion.1), channel_id=1, replica_groups=mesh['sub'=64,'crs'=4] {'sub','crs'}, use_global_device_ids=true, to_apply=%region_2.3 | all-reduce | flops 768 | bytes 6144 | tf_op jit(solution)/shard_map/psum | solution.py:79
  233.2 0.1 dynamic_slice.7
  233.2 0.0 copy-done.3
  233.2 0.4 convolution_reduce_fusion
  233.7 6.7 %psum.22 = f32[768]{0:T(1024)S(1)} all-reduce(f32[768]{0:T(1024)S(1)} %convolution_reduce_fusion), channel_id=1, replica_groups=mesh['sub'=64,'crs'=4] {'crs'}, use_global_device_ids=true, to_apply=%region_3.4 | all-reduce | flops 768 | bytes 6144 | tf_op jit(solution)/shard_map/psum | solution.py:84
  240.4 0.5 fusion
  240.9 0.3 fusion.7
  241.3 0.6 reshape.69
  241.9 0.0 all-gather.5.cloned.1.call-update
  242.0 76.1 %all-gather.5.cloned.1.call-done = f32[1536,768]{1,0:T(8,128)} async-done(((f32[24,768]{1,0:T(8,128)}), f32[1536,768]{1,0:T(8,128)}) %all-gather.5.cloned.1.call-update) | async-done | bytes 4718608 | tf_op jit(solution)/shard_map/all_gather | solution.py:93
  318.1 3.0 gather_fusion.2
  321.1 0.7 multiply_reduce_fusion
  321.7 0.7 copy.52
  322.4 75.2 %psum.23 = f32[1]{0:T(128)} all-reduce(f32[1]{0:T(128)} %bitcast.19), channel_id=1, replica_groups=mesh['sub'=64,'crs'=4] {'sub','crs'}, use_global_device_ids=true, to_apply=%region_5.6 | all-reduce | flops 1 | bytes 8 | tf_op jit(solution)/shard_map/psum | solution.py:96
  (17 shorter events, 0.2 us)
Async XLA Ops:
  7.2 149.2 %copy-start = (bf16[4,24,6,768]{3,1,2,0:T(8,128)(2,1)S(1)}, bf16[4,24,6,768]{3,1,2,0:T(8,128)(2,1)}, u32[]{:S(2)}) copy-start(bf16[4,24,6,768]{3,1,2,0:T(8,128)(2,1)} %param.13) | copy-start | bytes 2654212
  10.6 13.4 %copy-start.1 = (f32[4,6,768]{2,0,1:T(4,128)S(1)}, f32[4,6,768]{2,0,1:T(4,128)}, u32[]{:S(2)}) copy-start(f32[4,6,768]{2,0,1:T(4,128)} %param.9) | copy-start | bytes 221188
  10.7 14.1 %copy-start.5 = (s32[256]{0:T(256)S(1)}, s32[256]{0:T(256)}, u32[]{:S(2)}) copy-start(s32[256]{0:T(256)} %param.14) | copy-start | bytes 3076
  10.7 14.8 %copy-start.7 = (s32[6]{0:T(128)S(1)}, s32[6]{0:T(128)}, u32[]{:S(2)}) copy-start(s32[6]{0:T(128)} %constant.113.clone) | copy-start | bytes 76
  10.7 15.2 %copy-start.4 = (s32[4,6,4]{1,2,0:T(4,128)S(1)}, s32[4,6,4]{1,2,0:T(4,128)}, u32[]{:S(2)}) copy-start(s32[4,6,4]{1,2,0:T(4,128)} %param.11) | copy-start | bytes 1156
  10.7 134.3 %all-to-all-start = ((f32[64,24,768]{2,1,0:T(8,128)}), f32[64,24,768]{2,1,0:T(8,128)}, u32[]{:S(2)}, u32[]{:S(2)}) async-start(f32[64,24,768]{2,1,0:T(8,128)} %stack.24), calls=%async_computation | async-start | bytes 9437184 | tf_op jit(solution)/shard_map/all_to_all | solution.py:55
  24.0 124.0 %all-gather.3.cloned.1.call-start = ((), (), s32[]{:S(2)}) async-start(), calls=%async_computation.1 | async-start | bytes 4792320 | tf_op jit(solution)/shard_map/all_gather | solution.py:53
  24.7 293.4 %all-gather.5.cloned.1.call-start = ((), (), s32[]{:S(2)}) async-start(), calls=%async_computation.2 | async-start | bytes 4792320 | tf_op jit(solution)/shard_map/all_gather | solution.py:93
  26.2 11.4 %copy-start.6 = (s32[4,8]{1,0:T(4,128)S(1)}, s32[4,8]{1,0:T(4,128)}, u32[]{:S(2)}) copy-start(s32[4,8]{1,0:T(4,128)} %param.15) | copy-start | bytes 388
  26.2 124.7 %copy-start.2 = (f32[4,6,768]{2,0,1:T(4,128)S(1)}, f32[4,6,768]{2,0,1:T(4,128)}, u32[]{:S(2)}) copy-start(f32[4,6,768]{2,0,1:T(4,128)} %param.10) | copy-start | bytes 221188
  151.1 82.1 %copy-start.3 = (f32[192,768]{1,0:T(8,128)S(1)}, f32[192,768]{1,0:T(8,128)}, u32[]{:S(2)}) copy-start(f32[192,768]{1,0:T(8,128)} %param.16) | copy-start | bytes 1769476
Sparse Core Ops, SparseCore 0:
  28.1 104.1 all-gather.2
  242.1 75.9 all-gather.4
